TPU v7x, 32 devices: a whole 2x2x4 slice. The times are simulated.
32 devices in a mesh: grp: 4 (over z), row: 2 (over y), col: 4 (over x, core).
Axes of the slice: x: 2, y: 2, z: 4, core: 2. Of those that a mesh axis runs over, the one named last changes fastest.
Arguments:
- amplitudes: bfloat16 [1024, 16384], P(('grp', 'row'), 'col'), may hold values from -6 to 6
- ladder_ints: bfloat16 [16384, 16384], P('col', ('grp', 'row')), may hold values from -0.0625 to 0.0625
- tile_live: int32 [128, 128], P('col', ('grp', 'row')), may hold values 0 or 1
- cycle_direct: bfloat16 [4096, 4096], P('col', ('grp', 'row')), may hold values from -0.0625 to 0.0625
- cycle_exchange: bfloat16 [4096, 4096], P('col', ('grp', 'row')), may hold values from -0.0625 to 0.0625
- eps_occ: float32 [32], replicated, may hold values from -2 to -0.5
- eps_vir: float32 [128], replicated, may hold values from 0.5 to 3
Outputs:
- update: bfloat16 [1024, 16384], P('col', ('grp', 'row'))
All inputs are finite; a program needn't handle non-finite values. No bound on the sum of `tile_live` on one device may be relied on, other than what follows from the above.
Results may differ from a plain program's by a relative error of at most 0.001.
Values may be sent and summed in bfloat16 or wider, within the bound.
A program may use at most 128 MiB of HBM per device.

v0:
```python
import jax
import jax.numpy as jnp
from jax import lax
from jax.sharding import PartitionSpec as P


def body(amplitudes, ladder_ints, tile_live, cycle_direct, cycle_exchange, eps_occ, eps_vir):
    groups = lax.axis_size(("grp", "row"))
    columns = lax.axis_size("col")
    grp_count = lax.axis_size("grp")
    row_count = lax.axis_size("row")
    occ = eps_occ.shape[0]
    vir = eps_vir.shape[0]
    per_dev = occ // groups
    tile_edge = ladder_ints.shape[0] // tile_live.shape[0]
    expanded = jnp.repeat(jnp.repeat(tile_live, tile_edge, axis=0), tile_edge, axis=1).astype(
        jnp.bfloat16
    )
    masked = ladder_ints * expanded
    ladder = jnp.dot(
        lax.all_gather(amplitudes, ("grp", "row"), axis=0, tiled=True),
        masked,
        preferred_element_type=jnp.float32,
    )
    ladder = lax.psum_scatter(ladder, "col", scatter_dimension=0, tiled=True)
    width = amplitudes.shape[1]
    local = amplitudes.reshape(per_dev, grp_count, row_count, per_dev, width)
    local = local.transpose(0, 2, 1, 3, 4).reshape(per_dev, row_count, grp_count * per_dev, width)
    quarter = lax.all_to_all(local, "row", split_axis=1, concat_axis=0, tiled=True)
    k_count = row_count * per_dev
    j_count = grp_count * per_dev
    quarter = quarter.reshape(k_count, j_count, width)
    whole = lax.all_gather(quarter, "col", axis=2, tiled=True)
    amp_four = whole.reshape(k_count, j_count, vir, vir)
    u_one = amp_four.transpose(0, 2, 1, 3).reshape(k_count * vir, j_count * vir)
    u_two = amp_four.transpose(0, 3, 1, 2).reshape(k_count * vir, j_count * vir)
    total = jnp.dot(
        lax.all_gather(cycle_direct, "row", axis=1, tiled=True),
        u_one,
        preferred_element_type=jnp.float32,
    )
    partial_value = total + jnp.dot(
        lax.all_gather(cycle_exchange, "row", axis=1, tiled=True),
        u_two,
        preferred_element_type=jnp.float32,
    )
    cycle = lax.psum_scatter(partial_value, "grp", scatter_dimension=1, tiled=True)
    i_count = occ // columns
    a_count = vir // groups
    arranged = cycle.reshape(i_count, vir, per_dev, vir)
    arranged = lax.all_to_all(arranged, ("grp", "row"), split_axis=1, concat_axis=2, tiled=True)
    cycle_pairs = arranged.transpose(0, 2, 1, 3).reshape(i_count * occ, a_count * vir)
    occ_local = lax.dynamic_slice_in_dim(eps_occ, lax.axis_index("col") * i_count, i_count)
    vir_local = lax.dynamic_slice_in_dim(eps_vir, lax.axis_index(("grp", "row")) * a_count, a_count)
    denom = (
        vir_local[None, None, :, None]
        + eps_vir[None, None, None, :]
        - occ_local[:, None, None, None]
        - eps_occ[None, :, None, None]
    ).reshape(i_count * occ, a_count * vir)
    return ((ladder + cycle_pairs) / denom).astype(jnp.bfloat16)


def solution(mesh):
    placed = (
        P(("grp", "row"), "col"),
        P("col", ("grp", "row")),
        P("col", ("grp", "row")),
        P("col", ("grp", "row")),
        P("col", ("grp", "row")),
        P(),
        P(),
    )
    return jax.shard_map(
        body, mesh=mesh, in_specs=placed, out_specs=P("col", ("grp", "row")), check_vma=False
    )
```

profile of v0, /device:TPU:0, one launch (start us, length us, event | category | flops | bytes accessed | tf_op | source)
XLA Modules:
  0.0 490.0 jit_solution(15822599307230013603)
XLA Ops:
  6.5 1.5 reshape.72
  9.7 18.4 %all_to_all.33 = bf16[4,2,16,4096]{3,2,0,1:T(8,128)(2,1)} all-to-all(bf16[4,2,16,4096]{3,2,0,1:T(8,128)(2,1)S(1)} %copy.31), channel_id=1, replica_groups=mesh['grp'=4,'row'=2,'col'=4] {'row'}, dimensions={1} | all-to-all | bytes 2097152 | tf_op jit(solution)/shard_map/all_to_all | solution.py:29
  30.2 33.0 %all-gather.9.cloned.1.call-done = bf16[8,16,16384]{2,1,0:T(8,128)(2,1)} async-done(((bf16[8,16,4096]{2,1,0:T(8,128)(2,1)}), bf16[8,16,16384]{2,1,0:T(8,128)(2,1)}) %all-gather.9.cloned.1.call-update) | async-done | bytes 4194320 | tf_op jit(solution)/shard_map/all_gather | solution.py:33
  63.2 5.4 %copy.43 = bf16[16,8,128,128]{3,2,1,0:T(8,128)(2,1)} copy(bf16[16,8,128,128]{3,1,2,0:T(8,128)(2,1)} %bitcast.60) | data formatting | bytes 8388608
  68.6 6.8 %copy.33 = bf16[8,16,128,128]{2,1,3,0:T(8,128)(2,1)} copy(bf16[8,16,128,128]{3,2,1,0:T(8,128)(2,1)} %bitcast.61) | data formatting | bytes 8388608 | tf_op jit(solution)/shard_map/reshape | solution.py:34
  75.4 4.8 copy_bitcast_fusion
  80.3 17.6 %all-gather.11.cloned.1.call-done = bf16[1024,1024]{1,0:T(8,128)(2,1)} async-done(((bf16[1024,512]{1,0:T(8,128)(2,1)}), bf16[1024,1024]{1,0:T(8,128)(2,1)}) %all-gather.11.cloned.1.call-update) | async-done | bytes 2097168 | tf_op jit(solution)/shard_map/all_gather | solution.py:43
  97.9 10.9 %fusion.3 = f32[1024,2048]{1,0:T(8,128)} fusion(bf16[1024,1024]{1,0:T(8,128)(2,1)} %all-gather.11.cloned.1.call-done, bf16[128,8,16,128]{3,2,1,0:T(8,128)(2,1)} %bitcast.69), kind=kOutput, calls=%fused_computation.4 | convolution fusion | flops 4294967296 | bytes 14680064 | tf_op jit(solution)/shard_map/dot_general | solution.py:42
  108.8 23.8 %all-gather.7.cloned.1.call-done = bf16[1024,1024]{1,0:T(8,128)(2,1)} async-done(((bf16[1024,512]{1,0:T(8,128)(2,1)}), bf16[1024,1024]{1,0:T(8,128)(2,1)}) %all-gather.7.cloned.1.call-update) | async-done | bytes 2097168 | tf_op jit(solution)/shard_map/all_gather | solution.py:38
  132.6 13.1 %fusion.9 = f32[1024,2048]{1,0:T(8,128)} fusion(f32[1024,2048]{1,0:T(8,128)} %fusion.3, bf16[1024,1024]{1,0:T(8,128)(2,1)} %all-gather.7.cloned.1.call-done, bf16[128,8,16,128]{3,2,1,0:T(8,128)(2,1)} %bitcast.68), kind=kOutput, calls=%fused_computation.11 | convolution fusion | flops 4297064448 | bytes 23068672 | tf_op jit(solution)/shard_map/dot_general | solution.py:37
  146.5 112.6 %all-gather.5.cloned.1.call-done = bf16[1024,4096]{1,0:T(8,128)(2,1)} async-done(((bf16[128,4096]{1,0:T(8,128)(2,1)}), bf16[1024,4096]{1,0:T(8,128)(2,1)}) %all-gather.5.cloned.1.call-update) | async-done | bytes 8388624 | tf_op jit(solution)/shard_map/all_gather | solution.py:21
  259.2 17.9 %broadcast_in_dim.5 = bf16[4096,16,128]{2,1,0:T(8,128)(2,1)S(1)} broadcast(bf16[4096,16]{1,0:T(8,128)(2,1)S(1)} %bitcast.67), dimensions={0,1} | broadcast | bytes 16908288 | tf_op jit(solution)/shard_map/broadcast_in_dim | solution.py:16
  277.1 31.7 %fusion.2 = f32[1024,2048]{0,1:T(8,128)} fusion(bf16[1024,4096]{1,0:T(8,128)(2,1)} %all-gather.5.cloned.1.call-done, bf16[4096,2048]{1,0:T(8,128)(2,1)} %param.8, bf16[512,8,16,128]{3,2,1,0:T(8,128)(2,1)S(1)} %bitcast.59), kind=kOutput, calls=%fused_computation.3 | convolution fusion | flops 17188257792 | bytes 50331648 | tf_op jit(solution)/shard_map/dot_general | solution.py:20
  308.9 95.2 %reduce-scatter.5.cloned.1.call-done = f32[1024,512]{1,0:T(8,128)} async-done(((f32[1024,2048]{1,0:T(8,128)}), f32[1024,512]{1,0:T(8,128)}) %reduce-scatter.5.cloned.1.call-update) | async-done | bytes 2097168 | tf_op jit(solution)/shard_map/reduce_scatter | solution.py:47
  404.1 1.9 reshape.78
  406.1 1.9 copy.34
  408.0 5.2 %all-to-all-start.1 = ((f32[8,128,4,128]{3,2,0,1:T(4,128)}), f32[8,128,4,128]{3,2,0,1:T(4,128)S(1)}, u32[]{:S(2)}, u32[]{:S(2)}) async-start(f32[8,128,4,128]{3,2,0,1:T(4,128)} %copy.34), calls=%async_computation.3 | async-start | bytes 4194304 | tf_op jit(solution)/shard_map/all_to_all | solution.py:51
  413.7 2.3 copy.66
  416.0 3.5 copy.38
  419.6 41.8 %all-to-all-done.1 = f32[8,128,4,128]{3,2,0,1:T(4,128)S(1)} async-done(((f32[8,128,4,128]{3,2,0,1:T(4,128)}), f32[8,128,4,128]{3,2,0,1:T(4,128)S(1)}, u32[]{:S(2)}, u32[]{:S(2)}) %all-to-all-start.1) | async-done | bytes 2097184 | tf_op jit(solution)/shard_map/all_to_all | solution.py:51
  463.8 1.9 copy.37
  465.7 12.7 %reduce-scatter.3.cloned.1.call-done = f32[256,2048]{0,1:T(8,128)} async-done(((f32[1024,2048]{0,1:T(8,128)}), f32[256,2048]{0,1:T(8,128)}) %reduce-scatter.3.cloned.1.call-update) | async-done | bytes 2097168 | tf_op jit(solution)/shard_map/reduce_scatter | solution.py:25
  478.4 3.3 divide_convert_fusion
  481.7 1.4 copy.39
  (33 shorter events, 7.6 us)
Async XLA Ops:
  6.5 56.7 %all-gather.9.cloned.1.call-start = ((), (), s32[]{:S(2)}) async-start(), calls=%async_computation.7 | async-start | bytes 5242880 | tf_op jit(solution)/shard_map/all_gather | solution.py:33
  28.1 69.8 %all-gather.11.cloned.1.call-start = ((), (), s32[]{:S(2)}) async-start(), calls=%async_computation.8 | async-start | bytes 3145728 | tf_op jit(solution)/shard_map/all_gather | solution.py:43
  28.8 103.8 %all-gather.7.cloned.1.call-start = ((), (), s32[]{:S(2)}) async-start(), calls=%async_computation.6 | async-start | bytes 3145728 | tf_op jit(solution)/shard_map/all_gather | solution.py:38
  29.6 229.5 %all-gather.5.cloned.1.call-start = ((), (), s32[]{:S(2)}) async-start(), calls=%async_computation.4 | async-start | bytes 9437184 | tf_op jit(solution)/shard_map/all_gather | solution.py:21
  30.1 374.0 %reduce-scatter.5.cloned.1.call-start = ((), (), s32[]{:S(2)}) async-start(), calls=%async_computation.9 | async-start | bytes 10485760 | tf_op jit(solution)/shard_map/reduce_scatter | solution.py:47
  145.7 0.7 copy-start
  145.7 332.7 %reduce-scatter.3.cloned.1.call-start = ((), (), s32[]{:S(2)}) async-start(), calls=%async_computation.5 | async-start | bytes 10485760 | tf_op jit(solution)/shard_map/reduce_scatter | solution.py:25
  406.0 7.2 %copy-start.2 = (f32[32]{0:T(128)S(1)}, f32[32]{0:T(128)}, u32[]{:S(2)}) copy-start(f32[32]{0:T(128)} %param.12) | copy-start | bytes 388
  406.0 7.3 %copy-start.1 = (f32[128]{0:T(128)S(1)}, f32[128]{0:T(128)}, u32[]{:S(2)}) copy-start(f32[128]{0:T(128)} %param.13) | copy-start | bytes 1540
  408.0 53.4 %all-to-all-start.1 = ((f32[8,128,4,128]{3,2,0,1:T(4,128)}), f32[8,128,4,128]{3,2,0,1:T(4,128)S(1)}, u32[]{:S(2)}, u32[]{:S(2)}) async-start(f32[8,128,4,128]{3,2,0,1:T(4,128)} %copy.34), calls=%async_computation.3 | async-start | bytes 4194304 | tf_op jit(solution)/shard_map/all_to_all | solution.py:51
Sparse Core Ops, SparseCore 0:
  28.2 34.9 all-gather.8
  64.8 33.0 all-gather.10
  99.5 33.0 all-gather.6
  134.6 124.4 all-gather.4
  261.3 142.7 reduce-scatter.4
  406.5 71.8 reduce-scatter.2
where the time goes:
time: 491 us; the launch traced here: 490 us
  waiting for transfers between devices  339 us (69%)
  matrix products  55.7 us (11%)
  local copies, waits for them, and re-layouts  54.5 us (11%)
  blocking collectives  18.4 us (4%)
  between operations  13.6 us (3%)
  starting transfers between devices  5.62 us (1%)
    all_gather x1, waiting for transfers between devices, body(): lax.all_gather(amplitudes, ('grp', 'row'), axis=0, tiled=True)  113 us
    reduce_scatter x1, waiting for transfers between devices, body(): lax.psum_scatter(partial_value, 'grp', scatter_dimension=1, tiled=True)  95.2 us
    all_to_all x1, waiting for transfers between devices, body(): lax.all_to_all(arranged, ('grp', 'row'), split_axis=1, concat_axis=2, til...  41.8 us
    all_gather x1, waiting for transfers between devices, body(): whole = lax.all_gather(quarter, 'col', axis=2, tiled=True)  33 us
    dot_general x1, matrix products, body(): jnp.dot(lax.all_gather(amplitudes, ('grp', 'row'), axis=0, tiled=True), m...  31.7 us
    all_gather x1, waiting for transfers between devices, body(): lax.all_gather(cycle_direct, 'row', axis=1, tiled=True)  23.8 us
    all_to_all x1, blocking collectives, body(): lax.all_to_all(local, 'row', split_axis=1, concat_axis=0, tiled=True)  18.4 us
    broadcast_in_dim x1, local copies, waits for them, and re-layouts, body(): jnp.repeat(jnp.repeat(tile_live, tile_edge, axis=0), tile_edge, axis=1)  17.9 us
  transfers between devices with their start and end apart: 7, of which 7 were waited for; matrix products, arithmetic and copies ran while one was open for 21% of the time, Pallas kernels for 0%

commit v1 on v0

v1 whole, which is shorter than its diff:
```python
import jax
import jax.numpy as jnp
from jax import lax
from jax.sharding import PartitionSpec as P


def body(amplitudes, ladder_ints, tile_live, cycle_direct, cycle_exchange, eps_occ, eps_vir):
    groups = lax.axis_size(("grp", "row"))
    columns = lax.axis_size("col")
    col = lax.axis_index("col")
    grp = lax.axis_index(("grp", "row"))
    occ = eps_occ.shape[0]
    vir = eps_vir.shape[0]
    per_dev = occ // groups
    i_count = occ // columns
    a_count = vir // groups
    c_count = vir // columns
    f32 = jnp.float32

    x = cycle_exchange.reshape(i_count, groups, a_count, per_dev * vir)
    x = lax.all_to_all(x, ("grp", "row"), split_axis=1, concat_axis=3, tiled=True)
    x = lax.all_gather(x.reshape(i_count * a_count, occ * vir), "col", axis=0, tiled=True)

    w = cycle_direct.reshape(i_count, groups, a_count, per_dev, columns, c_count)
    w = w.transpose(1, 4, 0, 2, 3, 5).reshape(groups * columns, i_count * a_count, per_dev * c_count)
    w = lax.all_to_all(w, ("grp", "row", "col"), split_axis=0, concat_axis=0, tiled=True)
    w = w.reshape(groups, columns * i_count * a_count, per_dev * c_count)
    w = w.transpose(1, 0, 2).reshape(occ * a_count, occ * c_count)

    amps = lax.all_gather(amplitudes, ("grp", "row"), axis=0, tiled=True)
    tile_edge = ladder_ints.shape[0] // tile_live.shape[0]
    expanded = jnp.repeat(jnp.repeat(tile_live, tile_edge, axis=0), tile_edge, axis=1).astype(
        jnp.bfloat16
    )
    ladder = jnp.dot(amps, ladder_ints * expanded, preferred_element_type=f32)

    four = amps.reshape(occ, occ, c_count, vir)
    u_one = four.transpose(0, 2, 1, 3).reshape(occ * c_count, occ * vir)
    u_two = four.transpose(1, 2, 0, 3).reshape(occ * c_count, occ * vir)
    direct = jnp.dot(w, u_one, preferred_element_type=f32)
    exchange = lax.dot_general(x, u_two, (((1,), (1,)), ((), ())), preferred_element_type=f32)
    exchange = exchange.reshape(occ * a_count, occ, 1, c_count)
    exchange = jnp.broadcast_to(exchange, (occ * a_count, occ, columns, c_count)).reshape(
        occ * a_count, occ, vir
    )
    own = lax.broadcasted_iota(jnp.int32, (1, 1, vir), 2) // c_count == col
    cycle = direct.reshape(occ * a_count, occ, vir) + jnp.where(own, exchange, 0.0)
    cycle = cycle.reshape(occ, a_count, occ, vir).transpose(0, 2, 1, 3).reshape(occ * occ, a_count * vir)
    total = lax.psum_scatter(ladder + cycle, "col", scatter_dimension=0, tiled=True)

    occ_local = lax.dynamic_slice_in_dim(eps_occ, col * i_count, i_count)
    vir_local = lax.dynamic_slice_in_dim(eps_vir, grp * a_count, a_count)
    denom = (
        vir_local[None, None, :, None]
        + eps_vir[None, None, None, :]
        - occ_local[:, None, None, None]
        - eps_occ[None, :, None, None]
    ).reshape(i_count * occ, a_count * vir)
    return (total / denom).astype(jnp.bfloat16)


def solution(mesh):
    placed = (
        P(("grp", "row"), "col"),
        P("col", ("grp", "row")),
        P("col", ("grp", "row")),
        P("col", ("grp", "row")),
        P("col", ("grp", "row")),
        P(),
        P(),
    )
    return jax.shard_map(
        body, mesh=mesh, in_specs=placed, out_specs=P("col", ("grp", "row")), check_vma=False
    )
```

time: 491 us -> 437 us (0.89); the launches traced: 490 us -> 431 us
  waiting for transfers between devices: 339 us -> 150 us
  local copies, waits for them, and re-layouts: 54.5 us -> 156 us
  blocking collectives: 18.4 us -> 56.7 us
  matrix products: 55.7 us -> 48.2 us
    all_gather x4 -> x2, waiting for transfers between devices: 187 us -> 31.1 us  [the longest x1 31.1 us: body(): amps = lax.all_gather(amplitudes, ('grp', 'row'), axis=0, tiled=True)]
    reshape x8 -> x10, local copies, waits for them, and re-layouts: 20.6 us -> 65.6 us  [the longest x2 27.1 us: body(): four = amps.reshape(occ, occ, c_count, vir)]
    reduce_scatter x2 -> x1, waiting for transfers between devices: 108 us -> 65.2 us  [body(): lax.psum_scatter(ladder + cycle, 'col', scatter_dimension=0, tiled=True)]
    all_to_all x1, blocking collectives: 18.4 us -> 56.7 us  [body(): lax.all_to_all(x, ('grp', 'row'), split_axis=1, concat_axis=3, tiled=True)]
    unnamed x9 -> x17, local copies, waits for them, and re-layouts: 8.98 us -> 36.9 us
    another operation x0 -> x1, local copies, waits for them, and re-layouts: none -> 13.3 us
    dot_general x0 -> x1, local copies, waits for them, and re-layouts: none -> 12 us  [body(): direct = jnp.dot(w, u_one, preferred_element_type=f32)]
    all_to_all x1, waiting for transfers between devices: 41.8 us -> 53.1 us  [body(): lax.all_to_all(w, ('grp', 'row', 'col'), split_axis=0, concat_axis=0, til...]
  transfers between devices with their start and end apart: 7 -> 4, of which waited for: 7 -> 3; matrix products, arithmetic and copies ran while one was open for 21% -> 18% of each run, Pallas kernels for 0% -> 0%
where the time goes in v1:
time: 437 us; the launch traced here: 431 us
  local copies, waits for them, and re-layouts  156 us (36%)
  waiting for transfers between devices  150 us (34%)
  blocking collectives  56.7 us (13%)
  matrix products  48.2 us (11%)
  between operations  13.8 us (3%)
    reduce_scatter x1, waiting for transfers between devices, body(): lax.psum_scatter(ladder + cycle, 'col', scatter_dimension=0, tiled=True)  65.2 us
    all_to_all x1, blocking collectives, body(): lax.all_to_all(x, ('grp', 'row'), split_axis=1, concat_axis=3, tiled=True)  56.7 us
    all_to_all x1, waiting for transfers between devices, body(): lax.all_to_all(w, ('grp', 'row', 'col'), split_axis=0, concat_axis=0, til...  53.1 us
    unnamed x17, local copies, waits for them, and re-layouts  36.9 us
    dot_general x1, matrix products, body(): ladder = jnp.dot(amps, ladder_ints * expanded, preferred_element_type=f32)  31.5 us
    all_gather x1, waiting for transfers between devices, body(): amps = lax.all_gather(amplitudes, ('grp', 'row'), axis=0, tiled=True)  31.1 us
    reshape x2, local copies, waits for them, and re-layouts, body(): four = amps.reshape(occ, occ, c_count, vir)  27.1 us
    broadcast_in_dim x1, local copies, waits for them, and re-layouts, body(): jnp.repeat(jnp.repeat(tile_live, tile_edge, axis=0), tile_edge, axis=1)  19 us
  transfers between devices with their start and end apart: 4, of which 3 were waited for; matrix products, arithmetic and copies ran while one was open for 18% of the time, Pallas kernels for 0%

profile of v1, /device:TPU:0, one launch (start us, length us, event | category | flops | bytes accessed | tf_op | source)
XLA Modules:
  0.0 430.8 jit_solution(9802082074276299366)
XLA Ops:
  8.6 56.7 %all_to_all.20 = bf16[8,8,16,512]{3,2,0,1:T(8,128)(2,1)S(1)} all-to-all(bf16[8,8,16,512]{3,2,0,1:T(8,128)(2,1)S(1)} %copy.44), channel_id=1, replica_groups=mesh['grp'=4,'row'=2,'col'=4] {'grp','row'}, dimensions={1} | all-to-all | bytes 2097152 | tf_op jit(solution)/shard_map/all_to_all | solution.py:21
  67.3 3.8 reshape.132
  71.1 6.5 %copy.72 = bf16[8,8,16,4,4,32]{5,3,2,0,4,1:T(4,128)(2,1)} copy(bf16[8,8,16,4,4,32]{5,4,3,2,1,0:T(4,128)(2,1)} %reshape.132) | data formatting | bytes 2097152 | tf_op jit(solution)/shard_map/reshape | solution.py:24
  77.7 6.4 %reshape.133 = bf16[32,128,128]{2,1,0:T(8,128)(2,1)} reshape(bf16[8,4,8,16,4,32]{5,4,3,2,1,0:T(4,128)(2,1)} %bitcast.69) | data formatting | bytes 2097152 | tf_op jit(solution)/shard_map/reshape | solution.py:25
  84.0 3.4 all-to-all-start
  87.6 53.1 %all-to-all-done = bf16[32,128,128]{2,1,0:T(8,128)(2,1)S(1)} async-done(((bf16[32,128,128]{2,1,0:T(8,128)(2,1)}), bf16[32,128,128]{2,1,0:T(8,128)(2,1)S(1)}, u32[]{:S(2)}, u32[]{:S(2)}) %all-to-all-start) | async-done | bytes 1048608 | tf_op jit(solution)/shard_map/all_to_all | solution.py:26
  142.4 31.1 %all-gather.3.cloned.1.call-done = bf16[1024,4096]{1,0:T(8,128)(2,1)} async-done(((bf16[128,4096]{1,0:T(8,128)(2,1)}), bf16[1024,4096]{1,0:T(8,128)(2,1)}) %all-gather.3.cloned.1.call-update) | async-done | bytes 8388624 | tf_op jit(solution)/shard_map/all_gather | solution.py:30
  173.5 10.2 %copy.53 = bf16[128,8,32,128]{3,2,1,0:T(8,128)(2,1)} copy(bf16[128,8,32,128]{3,1,2,0:T(8,128)(2,1)} %bitcast.71) | data formatting | bytes 16777216
  183.7 16.3 %copy.71 = bf16[32,32,32,128]{3,0,2,1:T(8,128)(2,1)} copy(bf16[32,32,32,128]{3,2,1,0:T(8,128)(2,1)} %bitcast.61) | data formatting | bytes 16777216 | tf_op jit(solution)/shard_map/reshape | solution.py:37
  200.0 10.7 %copy.42 = bf16[32,32,32,128]{3,1,2,0:T(8,128)(2,1)} copy(bf16[32,32,32,128]{3,2,1,0:T(8,128)(2,1)} %bitcast.62) | data formatting | bytes 16777216 | tf_op jit(solution)/shard_map/reshape | solution.py:37
  210.8 13.3 %reshape.140 = bf16[32,32,4096]{2,1,0:T(8,128)(2,1)} reshape(bf16[32,32,32,128]{3,2,1,0:T(8,128)(2,1)} %bitcast.65) | data formatting | bytes 16777216 | tf_op jit(solution)/shard_map/reshape.61
  224.1 8.2 %fusion.2 = f32[512,32,32]{0,2,1:T(8,128)S(1)} fusion(bf16[32,32,4096]{2,1,0:T(8,128)(2,1)} %reshape.140, bf16[512,4096]{1,0:T(8,128)(2,1)} %all-gather.5.cloned.1.call-done), kind=kOutput, calls=%fused_computation.8 | convolution fusion | flops 4294967296 | bytes 14680064 | tf_op jit(solution)/shard_map/dot_general | solution.py:41
  232.3 4.3 broadcast_in_dim.30
  236.6 9.1 %copy.47 = f32[512,32,128]{2,0,1:T(8,128)} copy(f32[512,32,128]{0,2,1:T(8,128)} %bitcast.63) | data formatting | bytes 16777216 | tf_op jit(solution)/shard_map/reshape | solution.py:43
  245.8 15.1 %copy.70 = bf16[128,8,32,128]{3,1,2,0:T(8,128)(2,1)} copy(bf16[128,8,32,128]{3,2,1,0:T(8,128)(2,1)} %bitcast.64) | data formatting | bytes 16777216
  260.9 12.0 %copy.43 = bf16[4096,1024]{1,0:T(8,128)(2,1)} copy(bf16[4096,1024]{0,1:T(8,128)(2,1)} %bitcast.66) | data formatting | bytes 16777216 | tf_op jit(solution)/shard_map/dot_general | solution.py:40
  272.9 8.5 %select_add_fusion = f32[512,32,128]{2,0,1:T(8,128)S(1)} fusion(f32[512,32,128]{2,0,1:T(8,128)} %copy.47, pred[128]{0:T(512)(128)(4,1)S(1)} %fusion.4, bf16[512,1024,1]{1,0,2:T(8,128)(2,1)S(1)} %reshape.144, bf16[32,128,1024]{2,1,0:T(8,128)(2,1)} %bitcast.74), kind=kOutput, calls=%fused_computation.7 | convolution fusion | flops 4299161600 | bytes 26214528 | tf_op jit(solution)/shard_map/dot_general | solution.py:40
  282.5 7.3 %copy.69 = f32[128,8,16,128]{3,1,2,0:T(8,128)} copy(f32[128,8,16,128]{3,2,1,0:T(8,128)S(1)} %bitcast.67) | data formatting | bytes 16777216
  289.9 9.2 %copy.49 = f32[1024,2048]{0,1:T(8,128)} copy(f32[1024,2048]{1,0:T(8,128)} %bitcast.68) | data formatting | bytes 16777216 | tf_op jit(solution)/shard_map/reshape | solution.py:48
  299.3 19.0 %broadcast_in_dim.28 = bf16[4096,16,128]{2,1,0:T(8,128)(2,1)} broadcast(bf16[4096,16]{1,0:T(8,128)(2,1)S(1)} %bitcast.78), dimensions={0,1} | broadcast | bytes 16908288 | tf_op jit(solution)/shard_map/broadcast_in_dim | solution.py:32
  318.2 31.5 %bitcast_add_fusion = f32[1024,2048]{0,1:T(8,128)} fusion(f32[1024,2048]{0,1:T(8,128)S(1)} %bitcast.73, bf16[1024,4096]{1,0:T(8,128)(2,1)} %all-gather.3.cloned.1.call-done, bf16[4096,2048]{1,0:T(8,128)(2,1)} %param.8, bf16[512,8,16,128]{3,2,1,0:T(8,128)(2,1)} %bitcast.70), kind=kOutput, calls=%fused_computation.5 | convolution fusion | flops 17190354944 | bytes 58720256 | tf_op jit(solution)/shard_map/dot_general | solution.py:35
  350.8 2.2 copy.73
  353.0 2.0 copy.50
  355.2 65.2 %reduce-scatter.2.cloned.1.call-done = f32[256,2048]{0,1:T(8,128)} async-done(((f32[1024,2048]{0,1:T(8,128)}), f32[256,2048]{0,1:T(8,128)}) %reduce-scatter.2.cloned.1.call-update) | async-done | bytes 2097168 | tf_op jit(solution)/shard_map/reduce_scatter | solution.py:49
  (39 shorter events, 11.7 us)
Async XLA Ops:
  6.5 60.8 %copy-start = (bf16[1024,512]{1,0:T(8,128)(2,1)S(1)}, bf16[1024,512]{1,0:T(8,128)(2,1)}, u32[]{:S(2)}) copy-start(bf16[1024,512]{1,0:T(8,128)(2,1)} %param.10) | copy-start | bytes 3145732
  6.5 166.9 %all-gather.3.cloned.1.call-start = ((), (), s32[]{:S(2)}) async-start(), calls=%async_computation.3 | async-start | bytes 9437184 | tf_op jit(solution)/shard_map/all_gather | solution.py:30
  7.3 216.8 %all-gather.5.cloned.1.call-start = ((), (), s32[]{:S(2)}) async-start(), calls=%async_computation.4 | async-start | bytes 5242880 | tf_op jit(solution)/shard_map/all_gather | solution.py:22
  71.1 16.3 %copy-start.1 = (s32[32,16]{0,1:T(8,128)S(1)}, s32[32,16]{0,1:T(8,128)}, u32[]{:S(2)}) copy-start(s32[32,16]{0,1:T(8,128)} %param.9) | copy-start | bytes 6148
  84.0 56.7 %all-to-all-start = ((bf16[32,128,128]{2,1,0:T(8,128)(2,1)}), bf16[32,128,128]{2,1,0:T(8,128)(2,1)S(1)}, u32[]{:S(2)}, u32[]{:S(2)}) async-start(bf16[32,128,128]{2,1,0:T(8,128)(2,1)} %reshape.133), calls=%async_computation | async-start | bytes 2097152 | tf_op jit(solution)/shard_map/all_to_all | solution.py:26
  87.4 333.0 %reduce-scatter.2.cloned.1.call-start = ((), (), s32[]{:S(2)}) async-start(), calls=%async_computation.5 | async-start | bytes 10485760 | tf_op jit(solution)/shard_map/reduce_scatter | solution.py:49
  299.1 19.1 %slice-start = ((s8[8388608]{0:T(1024)(128)(4,1)}), s8[4194304]{0:T(1024)(128)(4,1)S(1)}, s32[]{:S(2)}) async-start(s8[8388608]{0:T(1024)(128)(4,1)} %bitcast.72), calls=%async_computation.6 | async-start | bytes 8388608
  299.2 19.0 %slice-start.1 = ((s8[8388608]{0:T(1024)(128)(4,1)}), s8[4194304]{0:T(1024)(128)(4,1)S(1)}, s32[]{:S(2)}) async-start(s8[8388608]{0:T(1024)(128)(4,1)} %bitcast.72), calls=%async_computation.7 | async-start | bytes 8388608
  349.7 0.7 copy-start.3
  349.7 0.7 copy-start.2
Sparse Core Ops, SparseCore 0:
  9.5 163.9 all-gather.2
  175.0 33.4 all-gather.4
  349.9 70.4 reduce-scatter.1

commit v2 on v1

--- a/solution.py
+++ b/solution.py
@@ -1,7 +1,90 @@
+import functools
+
 import jax
 import jax.numpy as jnp
 from jax import lax
+from jax.experimental import pallas as pl
+from jax.experimental.pallas import tpu as pltpu
 from jax.sharding import PartitionSpec as P
+
+LIMIT = 56 * 1024 * 1024
+
+
+def cycle_kernel(t_ref, w_ref, x_ref, o_ref):
+    occ, step, part, vir = t_ref.shape
+    col = lax.axis_index("col")
+    rows = w_ref.shape[0]
+    u_one = jnp.concatenate(
+        [t_ref[:, j].reshape(occ * part, vir) for j in range(step)], axis=1
+    )
+    direct = jnp.dot(w_ref[...], u_one, preferred_element_type=jnp.float32)
+    u_two = jnp.concatenate(
+        [t_ref[k].reshape(step * part, vir) for k in range(occ)], axis=1
+    )
+    exchange = lax.dot_general(
+        x_ref[...], u_two, (((1,), (1,)), ((), ())), preferred_element_type=jnp.float32
+    )
+    own = lax.broadcasted_iota(jnp.int32, (rows, vir), 1) // part == col
+    for j in range(step):
+        piece = exchange[:, j * part : (j + 1) * part]
+        piece = jnp.concatenate([piece] * (vir // part), axis=1)
+        o_ref[j] = direct[:, j * vir : (j + 1) * vir] + jnp.where(own, piece, 0.0)
+
+
+def cycle_sum(four, w, x):
+    occ, _, part, vir = four.shape
+    rows = w.shape[0]
+    step = 8
+    return pl.pallas_call(
+        cycle_kernel,
+        grid=(occ // step,),
+        out_shape=jax.ShapeDtypeStruct((occ, rows, vir), jnp.float32),
+        in_specs=[
+            pl.BlockSpec((occ, step, part, vir), lambda n: (0, n, 0, 0)),
+            pl.BlockSpec(w.shape, lambda n: (0, 0)),
+            pl.BlockSpec(x.shape, lambda n: (0, 0)),
+        ],
+        out_specs=pl.BlockSpec((step, rows, vir), lambda n: (n, 0, 0)),
+        compiler_params=pltpu.CompilerParams(vmem_limit_bytes=LIMIT),
+    )(four, w, x)
+
+
+def ladder_kernel(live_ref, a_ref, v_ref, o_ref, held):
+    edge = v_ref.shape[0] // live_ref.shape[0]
+    across = v_ref.shape[1] // edge
+    n = pl.program_id(0)
+
+    @pl.when(pl.program_id(1) == 0)
+    def _():
+        @pl.loop(0, live_ref.shape[0])
+        def _(k):
+            at = pl.ds(pl.multiple_of(k * edge, edge), edge)
+            for b in range(across):
+                lanes = slice(b * edge, (b + 1) * edge)
+                live = live_ref[k, n * across + b].astype(jnp.float32)
+                held[at, lanes] = (v_ref[at, lanes].astype(jnp.float32) * live).astype(jnp.bfloat16)
+
+    o_ref[...] = jnp.dot(a_ref[...], held[...], preferred_element_type=jnp.float32)
+
+
+def ladder_sum(amps, ints, live):
+    rows, depth = amps.shape
+    width = ints.shape[1]
+    tall = 256
+    wide = min(512, width)
+    return pl.pallas_call(
+        ladder_kernel,
+        grid=(width // wide, rows // tall),
+        out_shape=jax.ShapeDtypeStruct((rows, width), jnp.float32),
+        in_specs=[
+            pl.BlockSpec(memory_space=pltpu.SMEM),
+            pl.BlockSpec((tall, depth), lambda n, m: (m, 0)),
+            pl.BlockSpec((depth, wide), lambda n, m: (0, n)),
+        ],
+        out_specs=pl.BlockSpec((tall, wide), lambda n, m: (m, n)),
+        scratch_shapes=[pltpu.VMEM((depth, wide), jnp.bfloat16)],
+        compiler_params=pltpu.CompilerParams(vmem_limit_bytes=LIMIT),
+    )(live, amps, ints)
 
 
 def body(amplitudes, ladder_ints, tile_live, cycle_direct, cycle_exchange, eps_occ, eps_vir):
@@ -28,24 +111,9 @@
     w = w.transpose(1, 0, 2).reshape(occ * a_count, occ * c_count)
 
     amps = lax.all_gather(amplitudes, ("grp", "row"), axis=0, tiled=True)
-    tile_edge = ladder_ints.shape[0] // tile_live.shape[0]
-    expanded = jnp.repeat(jnp.repeat(tile_live, tile_edge, axis=0), tile_edge, axis=1).astype(
-        jnp.bfloat16
-    )
-    ladder = jnp.dot(amps, ladder_ints * expanded, preferred_element_type=f32)
-
-    four = amps.reshape(occ, occ, c_count, vir)
-    u_one = four.transpose(0, 2, 1, 3).reshape(occ * c_count, occ * vir)
-    u_two = four.transpose(1, 2, 0, 3).reshape(occ * c_count, occ * vir)
-    direct = jnp.dot(w, u_one, preferred_element_type=f32)
-    exchange = lax.dot_general(x, u_two, (((1,), (1,)), ((), ())), preferred_element_type=f32)
-    exchange = exchange.reshape(occ * a_count, occ, 1, c_count)
-    exchange = jnp.broadcast_to(exchange, (occ * a_count, occ, columns, c_count)).reshape(
-        occ * a_count, occ, vir
-    )
-    own = lax.broadcasted_iota(jnp.int32, (1, 1, vir), 2) // c_count == col
-    cycle = direct.reshape(occ * a_count, occ, vir) + jnp.where(own, exchange, 0.0)
-    cycle = cycle.reshape(occ, a_count, occ, vir).transpose(0, 2, 1, 3).reshape(occ * occ, a_count * vir)
+    ladder = ladder_sum(amps, ladder_ints, tile_live)
+    cycle = cycle_sum(amps.reshape(occ, occ, c_count, vir), w, x)
+    cycle = cycle.reshape(occ, occ, a_count, vir).transpose(1, 0, 2, 3).reshape(occ * occ, a_count * vir)
     total = lax.psum_scatter(ladder + cycle, "col", scatter_dimension=0, tiled=True)
 
     occ_local = lax.dynamic_slice_in_dim(eps_occ, col * i_count, i_count)

time: 437 us -> 365 us (0.84); the launches traced: 431 us -> 364 us
  local copies, waits for them, and re-layouts: 156 us -> 40.9 us
  Pallas kernels: 0 us -> 52 us
  matrix products: 48.2 us -> 0 us
  waiting for transfers between devices: 150 us -> 180 us
  other arithmetic: 2.13 us -> 17.6 us
    pallas_call x0 -> x2, Pallas kernels: none -> 52 us  [the longest x1 36.7 us: ladder_sum(): pl.pallas_call(ladder_kernel, grid=(width // wide, rows // tall), out_sha...]
    dot_general x3 -> x0, matrix products: 48.2 us -> none  [the longest x1 31.5 us: body(): ladder = jnp.dot(amps, ladder_ints * expanded, preferred_element_type=f32)]
    reshape x5 -> x0, local copies, waits for them, and re-layouts: 46.6 us -> none  [the longest x2 27.1 us: body(): four = amps.reshape(occ, occ, c_count, vir)]
    all_gather x1, waiting for transfers between devices: 0.01 us -> 24.9 us  [body(): lax.all_gather(x.reshape(i_count * a_count, occ * vir), 'col', axis=0, ti...]
    unnamed x17 -> x11, local copies, waits for them, and re-layouts: 36.9 us -> 12.9 us
    broadcast_in_dim x3 -> x0, local copies, waits for them, and re-layouts: 23.4 us -> none  [the longest x1 19 us: body(): jnp.repeat(jnp.repeat(tile_live, tile_edge, axis=0), tile_edge, axis=1)]
    add x0 -> x1, other arithmetic: none -> 13.7 us  [body(): ladder + cycle]
    another operation x1 -> x0, local copies, waits for them, and re-layouts: 13.3 us -> none
  transfers between devices with their start and end apart: 4 -> 4, of which waited for: 3 -> 4; matrix products, arithmetic and copies ran while one was open for 18% -> 9% of each run, Pallas kernels for 0% -> 0%
where the time goes in v2:
time: 365 us; the launch traced here: 364 us
  waiting for transfers between devices  180 us (49%)
  blocking collectives  56.7 us (16%)
  Pallas kernels  52 us (14%)
  local copies, waits for them, and re-layouts  40.9 us (11%)
  other arithmetic  17.6 us (5%)
  between operations  13.2 us (4%)
    reduce_scatter x1, waiting for transfers between devices, body(): lax.psum_scatter(ladder + cycle, 'col', scatter_dimension=0, tiled=True)  70.6 us
    all_to_all x1, blocking collectives, body(): lax.all_to_all(x, ('grp', 'row'), split_axis=1, concat_axis=3, tiled=True)  56.7 us
    all_to_all x1, waiting for transfers between devices, body(): lax.all_to_all(w, ('grp', 'row', 'col'), split_axis=0, concat_axis=0, til...  52.5 us
    pallas_call x1, Pallas kernels, ladder_sum(): pl.pallas_call(ladder_kernel, grid=(width // wide, rows // tall), out_sha...  36.7 us
    all_gather x1, waiting for transfers between devices, body(): amps = lax.all_gather(amplitudes, ('grp', 'row'), axis=0, tiled=True)  31.5 us
    all_gather x1, waiting for transfers between devices, body(): lax.all_gather(x.reshape(i_count * a_count, occ * vir), 'col', axis=0, ti...  24.9 us
    pallas_call x1, Pallas kernels, cycle_sum(): pl.pallas_call(cycle_kernel, grid=(occ // step,), out_shape=jax.ShapeDtyp...  15.3 us
    add x1, other arithmetic, body(): ladder + cycle  13.7 us
  transfers between devices with their start and end apart: 4, of which 4 were waited for; matrix products, arithmetic and copies ran while one was open for 9% of the time, Pallas kernels for 0%

profile of v2, /device:TPU:0, one launch (start us, length us, event | category | flops | bytes accessed | tf_op | source)
XLA Modules:
  0.0 364.0 jit_solution(17131083985045739341)
XLA Ops:
  6.5 0.7 all-gather.3.cloned.1.call-update
  7.3 1.3 copy.24
  8.6 56.7 %all_to_all.20 = bf16[8,8,16,512]{3,2,0,1:T(8,128)(2,1)S(1)} all-to-all(bf16[8,8,16,512]{3,2,0,1:T(8,128)(2,1)S(1)} %copy.24), channel_id=1, replica_groups=mesh['grp'=4,'row'=2,'col'=4] {'grp','row'}, dimensions={1} | all-to-all | bytes 2097152 | tf_op jit(solution)/shard_map/all_to_all | solution.py:104
  65.3 0.6 copy.25
  65.9 1.4 copy.29
  67.3 3.8 %reshape.72 = bf16[8,8,16,4,4,32]{5,4,3,2,1,0:T(4,128)(2,1)} reshape(bf16[1024,512]{1,0:T(8,128)(2,1)S(1)} %copy-done) | data formatting | bytes 2097152 | tf_op jit(solution)/shard_map/reshape | solution.py:107
  71.2 6.5 %copy.36 = bf16[8,8,16,4,4,32]{5,3,2,0,4,1:T(4,128)(2,1)} copy(bf16[8,8,16,4,4,32]{5,4,3,2,1,0:T(4,128)(2,1)} %reshape.72) | data formatting | bytes 2097152 | tf_op jit(solution)/shard_map/reshape | solution.py:107
  77.6 6.4 %reshape.73 = bf16[32,128,128]{2,1,0:T(8,128)(2,1)} reshape(bf16[8,4,8,16,4,32]{5,4,3,2,1,0:T(4,128)(2,1)} %bitcast.40) | data formatting | bytes 2097152 | tf_op jit(solution)/shard_map/reshape | solution.py:108
  84.0 3.3 all-to-all-start
  87.3 0.2 reduce-scatter.2.cloned.1.call-start
  87.6 0.7 copy.21.live_ref
  88.2 52.5 %all-to-all-done = bf16[32,128,128]{2,1,0:T(8,128)(2,1)S(1)} async-done(((bf16[32,128,128]{2,1,0:T(8,128)(2,1)}), bf16[32,128,128]{2,1,0:T(8,128)(2,1)S(1)}, u32[]{:S(2)}, u32[]{:S(2)}) %all-to-all-start) | async-done | bytes 1048608 | tf_op jit(solution)/shard_map/all_to_all | solution.py:109
  140.7 1.3 copy.37
  142.0 31.5 %all-gather.3.cloned.1.call-done.a_ref = bf16[1024,4096]{1,0:T(8,128)(2,1)} async-done(((bf16[128,4096]{1,0:T(8,128)(2,1)}), bf16[1024,4096]{1,0:T(8,128)(2,1)}) %all-gather.3.cloned.1.call-update) | async-done | bytes 8388624 | tf_op jit(solution)/shard_map/all_gather | solution.py:113
  173.5 10.2 %copy.28 = bf16[128,8,32,128]{3,2,1,0:T(8,128)(2,1)} copy(bf16[128,8,32,128]{3,1,2,0:T(8,128)(2,1)} %bitcast.39) | data formatting | bytes 16777216
  183.7 24.9 %all-gather.5.cloned.1.call-done.x_ref = bf16[512,4096]{1,0:T(8,128)(2,1)} async-done(((bf16[128,4096]{1,0:T(8,128)(2,1)}), bf16[512,4096]{1,0:T(8,128)(2,1)}) %all-gather.5.cloned.1.call-update) | async-done | bytes 4194320 | tf_op jit(solution)/shard_map/all_gather | solution.py:105
  208.6 15.3 %shard_map.74 = f32[32,512,128]{2,1,0:T(8,128)} custom-call(bf16[32,32,32,128]{3,2,1,0:T(8,128)(2,1)} %bitcast.37, bf16[512,1024]{1,0:T(8,128)(2,1)} %bitcast.46, bf16[512,4096]{1,0:T(8,128)(2,1)} %all-gather.5.cloned.1.call-done.x_ref), custom_call_target="tpu_custom_call" | custom-call | tf_op jit(solution)/shard_map/pallas_call | solution.py:38
  223.9 7.7 %copy.26 = f32[32,32,16,128]{3,2,1,0:T(8,128)} copy(f32[32,32,16,128]{3,2,0,1:T(8,128)} %bitcast.38) | data formatting | bytes 16777216 | tf_op jit(solution)/shard_map/transpose | solution.py:116
  231.6 36.7 %shard_map.73 = f32[1024,2048]{1,0:T(8,128)} custom-call(s32[32,16]{1,0:T(8,128)} %copy.21.live_ref, bf16[1024,4096]{1,0:T(8,128)(2,1)} %all-gather.3.cloned.1.call-done.a_ref, bf16[4096,2048]{1,0:T(8,128)(2,1)} %v_ref.1), custom_call_target="tpu_custom_call" | custom-call | tf_op jit(solution)/shard_map/pallas_call | solution.py:75
  268.3 13.7 %bitcast_add_fusion = f32[1024,2048]{1,0:T(8,128)} fusion(f32[1024,2048]{1,0:T(8,128)} %shard_map.73, f32[128,8,16,128]{3,2,1,0:T(8,128)} %bitcast.36), kind=kLoop, calls=%fused_computation | loop fusion | flops 2097152 | bytes 25165824 | tf_op jit(solution)/shard_map/add | solution.py:117
  282.0 0.6 copy-done.2
  283.0 70.6 %reduce-scatter.2.cloned.1.call-done = f32[256,2048]{1,0:T(8,128)} async-done(((f32[1024,2048]{1,0:T(8,128)}), f32[256,2048]{1,0:T(8,128)}) %reduce-scatter.2.cloned.1.call-update) | async-done | bytes 2097168 | tf_op jit(solution)/shard_map/reduce_scatter | solution.py:117
  353.6 0.2 sub.41
  353.8 3.8 %fusion.1 = bf16[256,2048]{1,0:T(8,128)(2,1)} fusion(f32[256,2048]{1,0:T(8,128)} %reduce-scatter.2.cloned.1.call-done, f32[32,8,16,128]{3,2,1,0:T(8,128)S(1)} %bitcast.41, f32[256]{0:T(256)S(1)} %sub.44), kind=kLoop, calls=%fused_computation.4 | loop fusion | flops 1572864 | bytes 5243904 | tf_op jit(solution)/shard_map/convert_element_type | solution.py:127
  (17 shorter events, 0.5 us)
Async XLA Ops:
  6.5 60.8 %copy-start = (bf16[1024,512]{1,0:T(8,128)(2,1)S(1)}, bf16[1024,512]{1,0:T(8,128)(2,1)}, u32[]{:S(2)}) copy-start(bf16[1024,512]{1,0:T(8,128)(2,1)} %param.10) | copy-start | bytes 3145732
  6.5 166.9 %all-gather.3.cloned.1.call-start = ((), (), s32[]{:S(2)}) async-start(), calls=%async_computation.3 | async-start | bytes 9437184 | tf_op jit(solution)/shard_map/all_gather | solution.py:113
  7.3 201.4 %all-gather.5.cloned.1.call-start = ((), (), s32[]{:S(2)}) async-start(), calls=%async_computation.4 | async-start | bytes 5242880 | tf_op jit(solution)/shard_map/all_gather | solution.py:105
  71.2 16.4 %copy-start.1 = (s32[32,16]{0,1:T(8,128)S(1)}, s32[32,16]{0,1:T(8,128)}, u32[]{:S(2)}) copy-start(s32[32,16]{0,1:T(8,128)} %param.9) | copy-start | bytes 6148
  84.0 56.7 %all-to-all-start = ((bf16[32,128,128]{2,1,0:T(8,128)(2,1)}), bf16[32,128,128]{2,1,0:T(8,128)(2,1)S(1)}, u32[]{:S(2)}, u32[]{:S(2)}) async-start(bf16[32,128,128]{2,1,0:T(8,128)(2,1)} %reshape.73), calls=%async_computation | async-start | bytes 2097152 | tf_op jit(solution)/shard_map/all_to_all | solution.py:109
  87.3 266.3 %reduce-scatter.2.cloned.1.call-start = ((), (), s32[]{:S(2)}) async-start(), calls=%async_computation.5 | async-start | bytes 10485760 | tf_op jit(solution)/shard_map/reduce_scatter | solution.py:117
  282.0 0.7 copy-start.2
  282.0 0.8 copy-start.3
Sparse Core Ops, SparseCore 0:
  9.5 163.9 all-gather.2
  175.0 33.5 all-gather.4
  282.1 71.4 reduce-scatter.1

commit v3 on v2

--- a/solution.py
+++ b/solution.py
@@ -112,6 +112,7 @@
 
     amps = lax.all_gather(amplitudes, ("grp", "row"), axis=0, tiled=True)
     ladder = ladder_sum(amps, ladder_ints, tile_live)
+    amps, ladder = lax.optimization_barrier((amps, ladder))
     cycle = cycle_sum(amps.reshape(occ, occ, c_count, vir), w, x)
     cycle = cycle.reshape(occ, occ, a_count, vir).transpose(1, 0, 2, 3).reshape(occ * occ, a_count * vir)
     total = lax.psum_scatter(ladder + cycle, "col", scatter_dimension=0, tiled=True)

time: 365 us -> 339 us (0.929)
  waiting for transfers between devices: 180 us -> 154 us
    all_gather x1, waiting for transfers between devices: 24.9 us -> 0.01 us  [body(): lax.all_gather(x.reshape(i_count * a_count, occ * vir), 'col', axis=0, ti...]
  transfers between devices with their start and end apart: 4 -> 4, of which waited for: 4 -> 3; matrix products, arithmetic and copies ran while one was open for 9% -> 9% of each run, Pallas kernels for 0% -> 11%
where the time goes in v3:
time: 339 us; the launch traced here: 338 us
  waiting for transfers between devices  154 us (45%)
  blocking collectives  56.7 us (17%)
  Pallas kernels  52.8 us (16%)
  local copies, waits for them, and re-layouts  40.1 us (12%)
  other arithmetic  17.6 us (5%)
  between operations  13.2 us (4%)
  starting transfers between devices  3.67 us (1%)
    reduce_scatter x1, waiting for transfers between devices, body(): lax.psum_scatter(ladder + cycle, 'col', scatter_dimension=0, tiled=True)  69.4 us
    all_to_all x1, blocking collectives, body(): lax.all_to_all(x, ('grp', 'row'), split_axis=1, concat_axis=3, tiled=True)  56.7 us
    all_to_all x1, waiting for transfers between devices, body(): lax.all_to_all(w, ('grp', 'row', 'col'), split_axis=0, concat_axis=0, til...  52.3 us
    pallas_call x1, Pallas kernels, ladder_sum(): pl.pallas_call(ladder_kernel, grid=(width // wide, rows // tall), out_sha...  37.5 us
    all_gather x1, waiting for transfers between devices, body(): amps = lax.all_gather(amplitudes, ('grp', 'row'), axis=0, tiled=True)  31.5 us
    pallas_call x1, Pallas kernels, cycle_sum(): pl.pallas_call(cycle_kernel, grid=(occ // step,), out_shape=jax.ShapeDtyp...  15.3 us
    add x1, other arithmetic, body(): ladder + cycle  13.7 us
    unnamed x11, local copies, waits for them, and re-layouts  12.2 us
  transfers between devices with their start and end apart: 4, of which 3 were waited for; matrix products, arithmetic and copies ran while one was open for 9% of the time, Pallas kernels for 11%

profile of v3, /device:TPU:0, one launch (start us, length us, event | category | flops | bytes accessed | tf_op | source)
XLA Modules:
  0.0 337.9 jit_solution(15654194350852980752)
XLA Ops:
  6.5 0.7 all-gather.3.cloned.1.call-update
  7.3 1.3 copy.24
  8.6 56.7 %all_to_all.20 = bf16[8,8,16,512]{3,2,0,1:T(8,128)(2,1)S(1)} all-to-all(bf16[8,8,16,512]{3,2,0,1:T(8,128)(2,1)S(1)} %copy.24), channel_id=1, replica_groups=mesh['grp'=4,'row'=2,'col'=4] {'grp','row'}, dimensions={1} | all-to-all | bytes 2097152 | tf_op jit(solution)/shard_map/all_to_all | solution.py:104
  65.3 0.6 copy.25
  65.9 1.5 copy.29
  67.4 3.8 %reshape.72 = bf16[8,8,16,4,4,32]{5,4,3,2,1,0:T(4,128)(2,1)} reshape(bf16[1024,512]{1,0:T(8,128)(2,1)S(1)} %copy-done) | data formatting | bytes 2097152 | tf_op jit(solution)/shard_map/reshape | solution.py:107
  71.3 6.5 %copy.36 = bf16[8,8,16,4,4,32]{5,3,2,0,4,1:T(4,128)(2,1)} copy(bf16[8,8,16,4,4,32]{5,4,3,2,1,0:T(4,128)(2,1)} %reshape.72) | data formatting | bytes 2097152 | tf_op jit(solution)/shard_map/reshape | solution.py:107
  77.7 6.4 %reshape.73 = bf16[32,128,128]{2,1,0:T(8,128)(2,1)} reshape(bf16[8,4,8,16,4,32]{5,4,3,2,1,0:T(4,128)(2,1)} %bitcast.40) | data formatting | bytes 2097152 | tf_op jit(solution)/shard_map/reshape | solution.py:108
  84.1 3.4 %all-to-all-start = ((bf16[32,128,128]{2,1,0:T(8,128)(2,1)}), bf16[32,128,128]{2,1,0:T(8,128)(2,1)S(1)}, u32[]{:S(2)}, u32[]{:S(2)}) async-start(bf16[32,128,128]{2,1,0:T(8,128)(2,1)} %reshape.73), calls=%async_computation | async-start | bytes 2097152 | tf_op jit(solution)/shard_map/all_to_all | solution.py:109
  87.5 0.2 reduce-scatter.2.cloned.1.call-start
  87.7 0.7 copy.21.live_ref
  88.4 52.3 %all-to-all-done = bf16[32,128,128]{2,1,0:T(8,128)(2,1)S(1)} async-done(((bf16[32,128,128]{2,1,0:T(8,128)(2,1)}), bf16[32,128,128]{2,1,0:T(8,128)(2,1)S(1)}, u32[]{:S(2)}, u32[]{:S(2)}) %all-to-all-start) | async-done | bytes 1048608 | tf_op jit(solution)/shard_map/all_to_all | solution.py:109
  140.7 1.3 copy.37
  142.0 31.5 %all-gather.3.cloned.1.call-done.a_ref = bf16[1024,4096]{1,0:T(8,128)(2,1)} async-done(((bf16[128,4096]{1,0:T(8,128)(2,1)}), bf16[1024,4096]{1,0:T(8,128)(2,1)}) %all-gather.3.cloned.1.call-update) | async-done | bytes 8388624 | tf_op jit(solution)/shard_map/all_gather | solution.py:113
  173.5 37.5 %shard_map.73 = f32[1024,2048]{1,0:T(8,128)} custom-call(s32[32,16]{1,0:T(8,128)} %copy.21.live_ref, bf16[1024,4096]{1,0:T(8,128)(2,1)} %all-gather.3.cloned.1.call-done.a_ref, bf16[4096,2048]{1,0:T(8,128)(2,1)} %v_ref.1), custom_call_target="tpu_custom_call" | custom-call | tf_op jit(solution)/shard_map/pallas_call | solution.py:75
  210.9 9.4 %copy.28 = bf16[128,8,32,128]{3,2,1,0:T(8,128)(2,1)} copy(bf16[128,8,32,128]{3,1,2,0:T(8,128)(2,1)} %bitcast.39) | data formatting | bytes 16777216
  220.4 15.3 %shard_map.74 = f32[32,512,128]{2,1,0:T(8,128)} custom-call(bf16[32,32,32,128]{3,2,1,0:T(8,128)(2,1)} %bitcast.37, bf16[512,1024]{1,0:T(8,128)(2,1)} %bitcast.46, bf16[512,4096]{1,0:T(8,128)(2,1)} %all-gather.5.cloned.1.call-done.x_ref), custom_call_target="tpu_custom_call" | custom-call | tf_op jit(solution)/shard_map/pallas_call | solution.py:38
  235.7 7.7 %copy.26 = f32[32,32,16,128]{3,2,1,0:T(8,128)} copy(f32[32,32,16,128]{3,2,0,1:T(8,128)} %bitcast.38) | data formatting | bytes 16777216 | tf_op jit(solution)/shard_map/transpose | solution.py:117
  243.4 13.7 %bitcast_add_fusion = f32[1024,2048]{1,0:T(8,128)} fusion(f32[1024,2048]{1,0:T(8,128)} %shard_map.73, f32[128,8,16,128]{3,2,1,0:T(8,128)} %bitcast.36), kind=kLoop, calls=%fused_computation | loop fusion | flops 2097152 | bytes 25165824 | tf_op jit(solution)/shard_map/add | solution.py:118
  257.1 0.6 copy-done.2
  257.8 0.1 sub.44
  258.1 69.4 %reduce-scatter.2.cloned.1.call-done = f32[256,2048]{1,0:T(8,128)} async-done(((f32[1024,2048]{1,0:T(8,128)}), f32[256,2048]{1,0:T(8,128)}) %reduce-scatter.2.cloned.1.call-update) | async-done | bytes 2097168 | tf_op jit(solution)/shard_map/reduce_scatter | solution.py:118
  327.5 0.2 sub.41
  327.7 3.8 %fusion.1 = bf16[256,2048]{1,0:T(8,128)(2,1)} fusion(f32[256,2048]{1,0:T(8,128)} %reduce-scatter.2.cloned.1.call-done, f32[32,8,16,128]{3,2,1,0:T(8,128)S(1)} %bitcast.41, f32[256]{0:T(256)S(1)} %sub.44), kind=kLoop, calls=%fused_computation.4 | loop fusion | flops 1572864 | bytes 5243904 | tf_op jit(solution)/shard_map/convert_element_type | solution.py:128
  (17 shorter events, 0.4 us)
Async XLA Ops:
  6.5 60.9 %copy-start = (bf16[1024,512]{1,0:T(8,128)(2,1)S(1)}, bf16[1024,512]{1,0:T(8,128)(2,1)}, u32[]{:S(2)}) copy-start(bf16[1024,512]{1,0:T(8,128)(2,1)} %param.10) | copy-start | bytes 3145732
  6.5 166.9 %all-gather.3.cloned.1.call-start = ((), (), s32[]{:S(2)}) async-start(), calls=%async_computation.3 | async-start | bytes 9437184 | tf_op jit(solution)/shard_map/all_gather | solution.py:113
  7.3 213.1 %all-gather.5.cloned.1.call-start = ((), (), s32[]{:S(2)}) async-start(), calls=%async_computation.4 | async-start | bytes 5242880 | tf_op jit(solution)/shard_map/all_gather | solution.py:105
  71.2 16.5 %copy-start.1 = (s32[32,16]{0,1:T(8,128)S(1)}, s32[32,16]{0,1:T(8,128)}, u32[]{:S(2)}) copy-start(s32[32,16]{0,1:T(8,128)} %param.9) | copy-start | bytes 6148
  84.1 56.6 %all-to-all-start = ((bf16[32,128,128]{2,1,0:T(8,128)(2,1)}), bf16[32,128,128]{2,1,0:T(8,128)(2,1)S(1)}, u32[]{:S(2)}, u32[]{:S(2)}) async-start(bf16[32,128,128]{2,1,0:T(8,128)(2,1)} %reshape.73), calls=%async_computation | async-start | bytes 2097152 | tf_op jit(solution)/shard_map/all_to_all | solution.py:109
  87.5 240.0 %reduce-scatter.2.cloned.1.call-start = ((), (), s32[]{:S(2)}) async-start(), calls=%async_computation.5 | async-start | bytes 10485760 | tf_op jit(solution)/shard_map/reduce_scatter | solution.py:118
  257.1 0.7 copy-start.2
  257.1 0.8 copy-start.3
Sparse Core Ops, SparseCore 0:
  9.5 163.9 all-gather.2
  175.0 33.5 all-gather.4
  257.2 70.2 reduce-scatter.1
